TPU v7x, 768 devices: a whole 4x8x12 slice. The times are simulated.
768 devices in a mesh: tile: 32 (over x, z_lo, core), spec: 24 (over y, z_hi).
Axes of the slice: x: 4, y: 8, z: 12 (z_hi: 3, z_lo: 4; z = z_hi * 4 + z_lo), core: 2. Of those that a mesh axis runs over, the one named last changes fastest.
Arguments:
- concentrations: float32 [192, 12288, 256], P('spec', 'tile'), may hold values from 0.1 to 4
- courant: float32 [12288, 256], P('tile'), may hold values from 0.05 to 0.95
- first_weight: bfloat16 [192, 512], replicated, may hold values from -0.4375 to 0.4375
- middle_weight: bfloat16 [512, 512], replicated, may hold values from -0.25 to 0.25
- last_weight: bfloat16 [512, 192], replicated, may hold values from -0.25 to 0.25
- active_blocks: int32 [32, 24, 16], P('tile', 'spec'), may hold values from 0 to 32, as said below
- dest_tile: int32 [32, 24, 16], P('tile', 'spec'), may hold values from 0 to 31, as said below
Outputs:
- chemistry_out: bfloat16 [192, 3145728], P(None, ('tile', 'spec'))
- load_share: float32 [32, 24], P('tile', 'spec')
Inputs may be any that keep to these rules, and one draw needn't show every extreme that they name: `active_blocks`: each device's entries name distinct blocks of its own 32; the value 32 marks an empty slot. `dest_tile`: A listed block's tile lies within 2 tiles of its home tile along the periodic order of tiles; an empty slot names the home tile. At most 2 blocks of one device name one other tile, and at most 8 listed blocks over all devices of one spec index name one tile; both bounds are reached in every draw.
All inputs are finite; a program needn't handle non-finite values.
Results may differ from a plain program's by a relative error of at most 0.0035.
Values may be sent and summed in bfloat16 or wider, within the bound.
A program may use at most 32 MiB of HBM per device.

v0:
```python
import jax
import jax.numpy as jnp
from jax import lax
from jax.sharding import PartitionSpec as P

BLK = 128
NB = 32
RECV = 8
NBR = 2


def from_behind(value, axis, steps):
    count = lax.axis_size(axis)
    pairs = [(source, (source + steps) % count) for source in range(count)]
    return lax.ppermute(value, axis, pairs)


def extended(x, sides, width):
    for axis, dim in sides:
        devices, length = (lax.axis_size(axis), x.shape[dim])
        up = [(i, (i + 1) % devices) for i in range(devices)]
        down = [(j, i) for i, j in up]
        last = lax.slice_in_dim(x, length - width, length, axis=dim)
        initial = lax.slice_in_dim(x, 0, width, axis=dim)
        before = lax.ppermute(last, axis, up)
        after = lax.ppermute(initial, axis, down)
        x = jnp.concatenate([before, x, after], axis=dim)
    return x


def advect(values, courants):
    centre = values[:, 1:-1]
    left_diff = centre - values[:, :-2]
    right_diff = values[:, 2:] - centre
    slopes = jnp.where(
        left_diff * right_diff > 0,
        jnp.sign(left_diff) * jnp.minimum(jnp.abs(left_diff), jnp.abs(right_diff)),
        0.0,
    )
    fluxes = courants * (centre + 0.5 * (1.0 - courants) * slopes)
    return centre[:, 1:] - fluxes[:, 1:] + fluxes[:, :-1]


def surrogate(inputs, first_weight, middle_weight, last_weight):
    first_layer = jax.nn.silu(
        jnp.dot(first_weight.T, inputs, preferred_element_type=jnp.float32)
    ).astype(jnp.bfloat16)
    second = jax.nn.silu(
        jnp.dot(middle_weight.T, first_layer, preferred_element_type=jnp.float32)
    ).astype(jnp.bfloat16)
    change = jnp.dot(last_weight.T, second, preferred_element_type=jnp.float32)
    return (inputs.astype(jnp.float32) + change).astype(jnp.bfloat16)


def shards(
    concentrations, courant, first_weight, middle_weight, last_weight, active_blocks, dest_tile
):
    species_dev, shard_len, level_cols = concentrations.shape
    before = from_behind(courant[shard_len - 1 :], "tile", 1)
    rates_ext = jnp.concatenate([before, courant], axis=0)
    swept_field = concentrations
    for repeat in range(2):
        padded = extended(swept_field, (("tile", 1),), 2)
        swept_field = advect(padded[:, : shard_len + 3], rates_ext)
    advected = swept_field.astype(jnp.bfloat16).reshape(species_dev, shard_len * level_cols)
    regrouped = lax.all_to_all(advected, "spec", split_axis=1, concat_axis=0, tiled=True)
    species = regrouped.shape[0]
    grid_cell_block_list = regrouped.reshape(species, NB, BLK)
    listing = active_blocks.reshape(-1)
    targets = dest_tile.reshape(-1)
    slot_total = listing.shape[0]
    is_valid = listing < NB
    select_table = listing[:, None] == jnp.arange(NB, dtype=jnp.int32)[None, :]
    tiles_total = lax.axis_size("tile")
    home_tile = lax.axis_index("tile")
    offsets = (targets - home_tile + tiles_total // 2) % tiles_total - tiles_total // 2
    distances = [step_by for step_by in range(1, NBR + 1)] + [
        -step_by for step_by in range(1, NBR + 1)
    ]
    resident_selection = select_table.astype(jnp.bfloat16)
    picked = jnp.einsum(
        "au,cud->cad", resident_selection, grid_cell_block_list, preferred_element_type=jnp.float32
    ).astype(jnp.bfloat16)
    refreshed_state = surrogate(
        picked.reshape(species, slot_total * BLK), first_weight, middle_weight, last_weight
    )
    refreshed_state = refreshed_state.reshape(species, slot_total, BLK)
    assigned_blocks = jnp.einsum(
        "zu,xzi->xui", resident_selection, refreshed_state, preferred_element_type=jnp.float32
    )
    covered = jnp.sum(resident_selection.astype(jnp.float32), axis=0)
    own_total = jnp.sum((is_valid & (offsets == 0)).astype(jnp.float32)).reshape(1)
    for distance in distances:
        named_count = jnp.sum((is_valid & (offsets == distance)).astype(jnp.float32)).reshape(1)
        own_total = own_total + from_behind(named_count, "tile", distance)
    load_share = (own_total / RECV).reshape(1, 1)
    new_blocks = jnp.where(
        covered[None, :, None] > 0.5, assigned_blocks.astype(jnp.bfloat16), grid_cell_block_list
    )
    return (new_blocks.reshape(species, NB * BLK), load_share)


def solution(mesh):
    in_specs = (
        P("spec", "tile", None),
        P("tile", None),
        P(),
        P(),
        P(),
        P("tile", "spec", None),
        P("tile", "spec", None),
    )
    out_specs = (P(None, ("tile", "spec")), P("tile", "spec"))
    return jax.shard_map(shards, mesh=mesh, in_specs=in_specs, out_specs=out_specs, check_vma=False)
```

profile of v0, /device:TPU:167, one launch (start us, length us, event | category | flops | bytes accessed | tf_op | source)
XLA Modules:
  0.0 150.2 jit_solution(9175730337388545549)
XLA Ops:
  0.6 0.0 copy-start
  0.6 0.8 slice.63
  1.4 4.5 %collective-permute-start = (f32[1,256]{1,0:T(1,128)S(1)}, f32[1,256]{1,0:T(1,128)S(1)}, u32[]{:S(2)}, u32[]{:S(2)}) collective-permute-start(f32[1,256]{1,0:T(1,128)S(1)} %slice.63), channel_id=1, source_target_pairs={{0,24},{24,48},{48,72},{72,96},{96,120},{120,144},{144,168},{168,1... | collective-permute-start | bytes 3080 | tf_op jit(solution)/shard_map/ppermute | solution.py:15
  6.0 0.9 fusion.38
  6.9 1.9 %collective-permute-start.1 = (f32[8,2,256]{2,1,0:T(2,128)S(1)}, f32[8,2,256]{2,1,0:T(2,128)S(1)}, u32[]{:S(2)}, u32[]{:S(2)}) collective-permute-start(f32[8,2,256]{2,1,0:T(2,128)S(1)} %get-tuple-element.10), channel_id=1, source_target_pairs={{0,24},{24,48},{48,72},{72,96},{96,120},{120,144},{144,168},{168,1... | collective-permute-start | bytes 49160 | tf_op jit(solution)/shard_map/ppermute | solution.py:25
  8.8 2.4 %collective-permute-start.2 = (f32[8,2,256]{2,1,0:T(2,128)S(1)}, f32[8,2,256]{2,1,0:T(2,128)S(1)}, u32[]{:S(2)}, u32[]{:S(2)}) collective-permute-start(f32[8,2,256]{2,1,0:T(2,128)S(1)} %get-tuple-element.9), channel_id=1, source_target_pairs={{24,0},{48,24},{72,48},{96,72},{120,96},{144,120},{168,144},{192,1... | collective-permute-start | bytes 49160 | tf_op jit(solution)/shard_map/ppermute | solution.py:26
  11.2 0.0 collective-permute-done
  11.2 1.1 pad_maximum_fusion.4
  12.3 0.0 collective-permute-done.1
  12.3 1.6 %collective-permute-done.2 = f32[8,2,256]{2,1,0:T(2,128)S(1)} collective-permute-done((f32[8,2,256]{2,1,0:T(2,128)S(1)}, f32[8,2,256]{2,1,0:T(2,128)S(1)}, u32[]{:S(2)}, u32[]{:S(2)}) %collective-permute-start.2) | collective-permute-done | bytes 16416 | tf_op jit(solution)/shard_map/ppermute | solution.py:26
  13.8 5.6 %add_multiply_fusion.1 = f32[8,385,256]{2,1,0:T(8,128)S(1)} fusion(f32[8,384,256]{2,1,0:T(8,128)} %param.7, f32[8,2,256]{2,1,0:T(2,128)S(1)} %collective-permute-done.1, f32[8,2,256]{2,1,0:T(2,128)S(1)} %collective-permute-done.2, f32[385,256]{1,0:T(8,128)S(1)} %get-tuple-element.12, f32[385,256]{1,0:T(8,128)S(1)} %get-tuple-element.11), kind=kLoop, calls=%fused_computation.24 | loop fusion | flops 12615680 | bytes 7120896 | tf_op jit(solution)/shard_map/mul | solution.py:40
  19.5 0.4 slice_add_fusion.1
  19.9 1.9 %collective-permute-start.3 = (f32[8,2,256]{2,1,0:T(2,128)S(1)}, f32[8,2,256]{2,1,0:T(2,128)S(1)}, u32[]{:S(2)}, u32[]{:S(2)}) collective-permute-start(f32[8,2,256]{2,1,0:T(2,128)S(1)} %get-tuple-element.8), channel_id=1, source_target_pairs={{0,24},{24,48},{48,72},{72,96},{96,120},{120,144},{144,168},{168,1... | collective-permute-start | bytes 49160 | tf_op jit(solution)/shard_map/ppermute | solution.py:25
  21.8 2.4 %collective-permute-start.4 = (f32[8,2,256]{2,1,0:T(2,128)S(1)}, f32[8,2,256]{2,1,0:T(2,128)S(1)}, u32[]{:S(2)}, u32[]{:S(2)}) collective-permute-start(f32[8,2,256]{2,1,0:T(2,128)S(1)} %get-tuple-element.7), channel_id=1, source_target_pairs={{24,0},{48,24},{72,48},{96,72},{120,96},{144,120},{168,144},{192,1... | collective-permute-start | bytes 49160 | tf_op jit(solution)/shard_map/ppermute | solution.py:26
  24.2 0.0 collective-permute-done.3
  24.3 4.6 %collective-permute-done.4 = f32[8,2,256]{2,1,0:T(2,128)S(1)} collective-permute-done((f32[8,2,256]{2,1,0:T(2,128)S(1)}, f32[8,2,256]{2,1,0:T(2,128)S(1)}, u32[]{:S(2)}, u32[]{:S(2)}) %collective-permute-start.4) | collective-permute-done | bytes 16416 | tf_op jit(solution)/shard_map/ppermute | solution.py:26
  28.9 2.5 %add_multiply_fusion = f32[8,385,256]{2,1,0:T(8,128)S(1)} fusion(f32[8,384,256]{2,1,0:T(8,128)S(1)} %slice_add_fusion.1, f32[8,2,256]{2,1,0:T(2,128)S(1)} %collective-permute-done.3, f32[8,2,256]{2,1,0:T(2,128)S(1)} %collective-permute-done.4, f32[385,256]{1,0:T(8,128)S(1)} %get-tuple-element.12, f32[385,256]{1,0:T(8,128)S(1)} %get-tuple-element.11), kind=kLoop, calls=%fused_computation.22 | loop fusion | flops 12615680 | bytes 7120896 | tf_op jit(solution)/shard_map/mul | solution.py:40
  31.4 1.7 %fusion.12 = bf16[8,384,256]{2,1,0:T(8,128)(2,1)} fusion(f32[8,385,256]{2,1,0:T(8,128)S(1)} %add_multiply_fusion, f32[8,384,256]{2,1,0:T(8,128)S(1)} %slice_add_fusion.1), kind=kLoop, calls=%fused_computation.27 | loop fusion | flops 2359296 | bytes 11010048 | tf_op jit(solution)/shard_map/convert_element_type | solution.py:65
  33.1 2.6 %all_to_all.12 = bf16[8,24,4096]{2,1,0:T(8,128)(2,1)S(1)} reshape(bf16[8,384,256]{2,1,0:T(8,128)(2,1)} %fusion.12) | data formatting | bytes 3145728 | tf_op jit(solution)/shard_map/all_to_all | solution.py:66
  35.7 0.0 copy-start.3
  35.7 0.0 copy-start.4
  35.7 2.0 %copy.9 = bf16[8,24,4096]{2,0,1:T(8,128)(2,1)} copy(bf16[8,24,4096]{2,1,0:T(8,128)(2,1)S(1)} %all_to_all.12) | data formatting | bytes 3145728 | tf_op jit(solution)/shard_map/all_to_all | solution.py:66
  37.7 16.8 %all-to-all-start = ((bf16[8,24,4096]{2,0,1:T(8,128)(2,1)}), bf16[8,24,4096]{2,0,1:T(8,128)(2,1)S(1)}, u32[]{:S(2)}, u32[]{:S(2)}) async-start(bf16[8,24,4096]{2,0,1:T(8,128)(2,1)} %copy.9), calls=%async_computation | async-start | bytes 3145728 | tf_op jit(solution)/shard_map/all_to_all | solution.py:66
  54.6 0.0 copy-start.5
  54.6 0.0 copy-done.3
  54.6 0.0 copy-done.4
  54.6 0.7 fusion.34
  55.3 2.5 %collective-permute-start.5 = (f32[1]{0:T(128)}, f32[1]{0:T(128)}, u32[]{:S(2)}, u32[]{:S(2)}) collective-permute-start(f32[1]{0:T(128)} %bitcast.10), channel_id=1, source_target_pairs={{0,24},{24,48},{48,72},{72,96},{96,120},{120,144},{144,168},{168,1... | collective-permute-start | bytes 20 | tf_op jit(solution)/shard_map/ppermute | solution.py:15
  57.8 7.2 %collective-permute-start.6 = (f32[1]{0:T(128)}, f32[1]{0:T(128)}, u32[]{:S(2)}, u32[]{:S(2)}) collective-permute-start(f32[1]{0:T(128)} %bitcast.11), channel_id=1, source_target_pairs={{0,48},{24,72},{48,96},{72,120},{96,144},{120,168},{144,192},{168,... | collective-permute-start | bytes 20 | tf_op jit(solution)/shard_map/ppermute | solution.py:15
  65.0 2.1 %collective-permute-start.7 = (f32[1]{0:T(128)}, f32[1]{0:T(128)}, u32[]{:S(2)}, u32[]{:S(2)}) collective-permute-start(f32[1]{0:T(128)} %bitcast.12), channel_id=1, source_target_pairs={{0,744},{24,0},{48,24},{72,48},{96,72},{120,96},{144,120},{168,144... | collective-permute-start | bytes 20 | tf_op jit(solution)/shard_map/ppermute | solution.py:15
  67.1 1.9 %collective-permute-start.8 = (f32[1]{0:T(128)}, f32[1]{0:T(128)}, u32[]{:S(2)}, u32[]{:S(2)}) collective-permute-start(f32[1]{0:T(128)} %bitcast.13), channel_id=1, source_target_pairs={{0,720},{24,744},{48,0},{72,24},{96,48},{120,72},{144,96},{168,120... | collective-permute-start | bytes 20 | tf_op jit(solution)/shard_map/ppermute | solution.py:15
  69.0 0.1 convert_reduce_fusion
  69.1 62.0 %collective-permute-done.5 = f32[1]{0:T(128)} collective-permute-done((f32[1]{0:T(128)}, f32[1]{0:T(128)}, u32[]{:S(2)}, u32[]{:S(2)}) %collective-permute-start.5) | collective-permute-done | bytes 36 | tf_op jit(solution)/shard_map/ppermute | solution.py:15
  132.3 0.0 collective-permute-done.6
  133.0 0.0 collective-permute-done.7
  133.7 0.0 collective-permute-done.8
  134.3 0.0 all-to-all-done
  134.3 0.0 copy-start.2
  134.3 1.1 copy-done.2
  135.5 1.7 %copy.10 = bf16[24,8,32,128]{3,2,1,0:T(8,128)(2,1)S(1)} copy(bf16[24,8,32,128]{3,1,2,0:T(8,128)(2,1)} %bitcast.88) | data formatting | bytes 3145728
  137.2 0.4 convolution_convert_fusion.1
  137.6 0.0 copy-start.6
  137.7 2.7 %fusion.6 = bf16[512,2048]{0,1:T(8,128)(2,1)} fusion(bf16[192,512]{1,0:T(8,128)(2,1)S(1)} %copy-done.5, bf16[24,8,16,128]{3,2,1,0:T(8,128)(2,1)S(1)} %bitcast.92), kind=kOutput, calls=%fused_computation.10 | convolution fusion | flops 407896064 | bytes 3080192 | tf_op jit(solution)/shard_map/dot_general | solution.py:46
  140.3 0.0 copy-done.6
  140.3 4.9 %fusion.18 = bf16[24,8,16,128]{3,1,2,0:T(8,128)(2,1)} fusion(bf16[512,192]{0,1:T(8,128)(2,1)S(1)} %copy-done.6, bf16[512,2048]{0,1:T(8,128)(2,1)} %fusion.6, bf16[512,512]{1,0:T(8,128)(2,1)S(1)} %copy-done, bf16[24,8,16,128]{3,2,1,0:T(8,128)(2,1)S(1)} %bitcast.93), kind=kOutput, calls=%fused_computation.39 | convolution fusion | flops 1482817536 | bytes 4390912 | tf_op jit(solution)/shard_map/dot_general | solution.py:51
  145.3 1.3 copy.12
  146.6 0.7 bitcast_select_fusion
  147.2 1.9 %copy.20 = bf16[24,8,32,128]{3,1,2,0:T(8,128)(2,1)} copy(bf16[24,8,32,128]{3,2,1,0:T(8,128)(2,1)S(1)} %bitcast.89) | data formatting | bytes 3145728
  (6 shorter events, 0.0 us)
Async XLA Ops:
  0.6 139.7 %copy-start = (bf16[512,512]{1,0:T(8,128)(2,1)S(1)}, bf16[512,512]{1,0:T(8,128)(2,1)}, u32[]{:S(2)}) copy-start(bf16[512,512]{1,0:T(8,128)(2,1)} %param.10) | copy-start | bytes 1572868
  1.4 9.8 %collective-permute-start = (f32[1,256]{1,0:T(1,128)S(1)}, f32[1,256]{1,0:T(1,128)S(1)}, u32[]{:S(2)}, u32[]{:S(2)}) collective-permute-start(f32[1,256]{1,0:T(1,128)S(1)} %slice.63), channel_id=1, source_target_pairs={{0,24},{24,48},{48,72},{72,96},{96,120},{120,144},{144,168},{168,1... | collective-permute-start | bytes 3080 | tf_op jit(solution)/shard_map/ppermute | solution.py:15
  6.9 5.4 %collective-permute-start.1 = (f32[8,2,256]{2,1,0:T(2,128)S(1)}, f32[8,2,256]{2,1,0:T(2,128)S(1)}, u32[]{:S(2)}, u32[]{:S(2)}) collective-permute-start(f32[8,2,256]{2,1,0:T(2,128)S(1)} %get-tuple-element.10), channel_id=1, source_target_pairs={{0,24},{24,48},{48,72},{72,96},{96,120},{120,144},{144,168},{168,1... | collective-permute-start | bytes 49160 | tf_op jit(solution)/shard_map/ppermute | solution.py:25
  8.8 5.1 %collective-permute-start.2 = (f32[8,2,256]{2,1,0:T(2,128)S(1)}, f32[8,2,256]{2,1,0:T(2,128)S(1)}, u32[]{:S(2)}, u32[]{:S(2)}) collective-permute-start(f32[8,2,256]{2,1,0:T(2,128)S(1)} %get-tuple-element.9), channel_id=1, source_target_pairs={{24,0},{48,24},{72,48},{96,72},{120,96},{144,120},{168,144},{192,1... | collective-permute-start | bytes 49160 | tf_op jit(solution)/shard_map/ppermute | solution.py:26
  13.8 5.6 %copy-start.1 = (f32[8,384,256]{2,1,0:T(8,128)S(1)}, f32[8,384,256]{2,1,0:T(8,128)}, u32[]{:S(2)}) copy-start(f32[8,384,256]{2,1,0:T(8,128)} %param.7) | copy-start | bytes 9437188
  19.9 4.3 %collective-permute-start.3 = (f32[8,2,256]{2,1,0:T(2,128)S(1)}, f32[8,2,256]{2,1,0:T(2,128)S(1)}, u32[]{:S(2)}, u32[]{:S(2)}) collective-permute-start(f32[8,2,256]{2,1,0:T(2,128)S(1)} %get-tuple-element.8), channel_id=1, source_target_pairs={{0,24},{24,48},{48,72},{72,96},{96,120},{120,144},{144,168},{168,1... | collective-permute-start | bytes 49160 | tf_op jit(solution)/shard_map/ppermute | solution.py:25
  21.8 7.1 %collective-permute-start.4 = (f32[8,2,256]{2,1,0:T(2,128)S(1)}, f32[8,2,256]{2,1,0:T(2,128)S(1)}, u32[]{:S(2)}, u32[]{:S(2)}) collective-permute-start(f32[8,2,256]{2,1,0:T(2,128)S(1)} %get-tuple-element.7), channel_id=1, source_target_pairs={{24,0},{48,24},{72,48},{96,72},{120,96},{144,120},{168,144},{192,1... | collective-permute-start | bytes 49160 | tf_op jit(solution)/shard_map/ppermute | solution.py:26
  35.7 18.9 %copy-start.3 = (s32[1,1,16]{2,1,0:T(1,128)S(1)}, s32[1,1,16]{2,1,0:T(1,128)}, u32[]{:S(2)}) copy-start(s32[1,1,16]{2,1,0:T(1,128)} %param.12) | copy-start | bytes 196
  35.7 18.9 %copy-start.4 = (s32[1,1,16]{2,1,0:T(1,128)S(1)}, s32[1,1,16]{2,1,0:T(1,128)}, u32[]{:S(2)}) copy-start(s32[1,1,16]{2,1,0:T(1,128)} %param.13) | copy-start | bytes 196
  37.7 96.6 %all-to-all-start = ((bf16[8,24,4096]{2,0,1:T(8,128)(2,1)}), bf16[8,24,4096]{2,0,1:T(8,128)(2,1)S(1)}, u32[]{:S(2)}, u32[]{:S(2)}) async-start(bf16[8,24,4096]{2,0,1:T(8,128)(2,1)} %copy.9), calls=%async_computation | async-start | bytes 3145728 | tf_op jit(solution)/shard_map/all_to_all | solution.py:66
  54.6 83.1 %copy-start.5 = (bf16[192,512]{1,0:T(8,128)(2,1)S(1)}, bf16[192,512]{1,0:T(8,128)(2,1)}, u32[]{:S(2)}) copy-start(bf16[192,512]{1,0:T(8,128)(2,1)} %param.9) | copy-start | bytes 589828
  55.3 75.8 %collective-permute-start.5 = (f32[1]{0:T(128)}, f32[1]{0:T(128)}, u32[]{:S(2)}, u32[]{:S(2)}) collective-permute-start(f32[1]{0:T(128)} %bitcast.10), channel_id=1, source_target_pairs={{0,24},{24,48},{48,72},{72,96},{96,120},{120,144},{144,168},{168,1... | collective-permute-start | bytes 20 | tf_op jit(solution)/shard_map/ppermute | solution.py:15
  57.8 74.5 %collective-permute-start.6 = (f32[1]{0:T(128)}, f32[1]{0:T(128)}, u32[]{:S(2)}, u32[]{:S(2)}) collective-permute-start(f32[1]{0:T(128)} %bitcast.11), channel_id=1, source_target_pairs={{0,48},{24,72},{48,96},{72,120},{96,144},{120,168},{144,192},{168,... | collective-permute-start | bytes 20 | tf_op jit(solution)/shard_map/ppermute | solution.py:15
  65.0 68.0 %collective-permute-start.7 = (f32[1]{0:T(128)}, f32[1]{0:T(128)}, u32[]{:S(2)}, u32[]{:S(2)}) collective-permute-start(f32[1]{0:T(128)} %bitcast.12), channel_id=1, source_target_pairs={{0,744},{24,0},{48,24},{72,48},{96,72},{120,96},{144,120},{168,144... | collective-permute-start | bytes 20 | tf_op jit(solution)/shard_map/ppermute | solution.py:15
  67.1 66.6 %collective-permute-start.8 = (f32[1]{0:T(128)}, f32[1]{0:T(128)}, u32[]{:S(2)}, u32[]{:S(2)}) collective-permute-start(f32[1]{0:T(128)} %bitcast.13), channel_id=1, source_target_pairs={{0,720},{24,744},{48,0},{72,24},{96,48},{120,72},{144,96},{168,120... | collective-permute-start | bytes 20 | tf_op jit(solution)/shard_map/ppermute | solution.py:15
  134.3 1.1 copy-start.2
  137.6 2.7 %copy-start.6 = (bf16[512,192]{0,1:T(8,128)(2,1)S(1)}, bf16[512,192]{0,1:T(8,128)(2,1)}, u32[]{:S(2)}) copy-start(bf16[512,192]{0,1:T(8,128)(2,1)} %param.11) | copy-start | bytes 589828
where the time goes:
time: 151 us; the launch traced here: 150 us
  waiting for transfers between devices  68.2 us (45%)
  starting transfers between devices  43.7 us (29%)
  local copies, waits for them, and re-layouts  12.3 us (8%)
  other arithmetic  12.1 us (8%)
  matrix products  8.71 us (6%)
  between operations  5.19 us (3%)
    ppermute x5, waiting for transfers between devices, from_behind(): return lax.ppermute(value, axis, pairs)  62 us
    ppermute x5, starting transfers between devices, from_behind(): return lax.ppermute(value, axis, pairs)  18.2 us
    all_to_all x1, starting transfers between devices, shards(): lax.all_to_all(advected, 'spec', split_axis=1, concat_axis=0, tiled=True)  16.8 us
    mul x2, other arithmetic, advect(): fluxes = courants * (centre + 0.5 * (1.0 - courants) * slopes)  8.08 us
    ppermute x2, waiting for transfers between devices, extended(): after = lax.ppermute(initial, axis, down)  6.2 us
    unnamed x17, local copies, waits for them, and re-layouts  6.06 us
    dot_general x1, matrix products, surrogate(): change = jnp.dot(last_weight.T, second, preferred_element_type=jnp.float32)  4.94 us
    ppermute x2, starting transfers between devices, extended(): after = lax.ppermute(initial, axis, down)  4.8 us
  transfers between devices with their start and end apart: 10, of which 3 were waited for; matrix products, arithmetic and copies ran while one was open for 2% of the time, Pallas kernels for 0%

commit v1 on v0

v1 whole, which is shorter than its diff:
```python
import functools

import jax
import jax.numpy as jnp
from jax import lax
from jax.experimental import pallas as pl
from jax.experimental.pallas import tpu as pltpu
from jax.sharding import PartitionSpec as P

BLK = 128
RECV = 8
NBR = 2
GROUPS = 8
PAD = 8
MESH = pl.DeviceIdType.MESH
F32 = jnp.float32
BF16 = jnp.bfloat16


def minmod(left, right):
    return jnp.maximum(jnp.minimum(left, right), 0.0) + jnp.minimum(jnp.maximum(left, right), 0.0)


def fused_silu(half):
    return (half + half * jnp.tanh(half)).astype(BF16)


def kernel(
    n_tile, n_spec, n_z, n_group,
    conc, courant, w1_hbm, w2_hbm, w3_hbm, active, dest,
    out, share,
    field, rate, half_rest, field_in, rate_in, send, recv, w1, w2, w1_t, w2_t, w3_t, counts, counts_in,
    load_sem, weight_sem, halo_send, halo_recv, count_send, count_recv, send_sem, recv_sem, own_sem,
):
    tile = lax.axis_index("tile")
    me = lax.axis_index("spec")
    my_y, my_z = me // n_z, me % n_z
    n_y = n_spec // n_z
    rows = conc.shape[1]
    deep = rows + 2 * PAD
    share_rows = rows // n_spec
    width = conc.shape[2]
    halves = width // BLK
    per_group = share_rows // n_group
    up, down = (tile + 1) % n_tile, (tile + n_tile - 1) % n_tile

    def partner(k):
        return ((my_y + k) % n_y) * n_z + (my_z + k) % n_z

    species = conc.shape[0]

    def load(s, carry):
        for c in range(halves):
            pltpu.make_async_copy(
                conc.at[s, :, pl.ds(c * BLK, BLK)], field.at[c, pl.ds(pl.multiple_of(s * deep + PAD, PAD), rows), :], load_sem.at[c]
            ).start()
        return carry

    lax.fori_loop(0, species, load, 0)
    loads = []
    for c in range(halves):
        loads.append(pltpu.make_async_copy(
            courant.at[:, pl.ds(c * BLK, BLK)], rate.at[c, pl.ds(PAD, rows), :], load_sem.at[halves + c]))
        loads[-1].start()
        whole = field.at[c, pl.ds(0, species * rows), :]
        loads.append(pltpu.make_async_copy(whole, whole, load_sem.at[c]))
    weights = [
        pltpu.make_async_copy(w1_hbm, w1, weight_sem.at[0]),
        pltpu.make_async_copy(w2_hbm, w2, weight_sem.at[1]),
        pltpu.make_async_copy(w3_hbm, w3_t, weight_sem.at[2]),
    ]
    for copy in weights:
        copy.start()

    barrier = pltpu.get_barrier_semaphore()

    def greet(k, carry):
        pl.semaphore_signal(barrier, inc=1, device_id={"spec": partner(k)}, device_id_type=MESH)
        return carry

    lax.fori_loop(1, n_spec, greet, 0)
    steps = [1, -1, 2, -2]
    for step in steps:
        pl.semaphore_signal(barrier, inc=1, device_id={"tile": (tile + step + n_tile) % n_tile}, device_id_type=MESH)

    named = [jnp.int32(0)] * 5
    for j in range(active.shape[0]):
        home = (dest[j] - tile + n_tile + n_tile // 2) % n_tile - n_tile // 2
        valid = active[j] < out.shape[1] // BLK
        for i, step in enumerate([0] + steps):
            named[i] = named[i] + jnp.where(valid & (home == step), 1, 0)
    for i in range(5):
        counts[i] = jnp.full(counts.shape[1:], named[i], jnp.int32)

    for copy in loads:
        copy.wait()
    for c in range(halves):
        half_rest[c, PAD : PAD + rows] = 0.5 * (1.0 - rate[c, PAD : PAD + rows])

    def advect(d):
        first = PAD + d * share_rows
        finished = []
        for c in range(halves):
            def value(i):
                return field[c, pl.ds(first + i, species, stride=deep), :]

            def rates(i):
                return rate[c, pl.ds(first + i, 1), :], half_rest[c, pl.ds(first + i, 1), :]

            def flux(i, mid, left, right):
                speed, rest = rates(i)
                return speed * (mid + rest * minmod(left, right))

            before, mid = value(-4), value(-3)
            left = mid - before
            flow, once = None, {}
            done = []
            previous, left2, flow2 = None, None, None
            for i in range(-3, share_rows + 1):
                after = value(i + 1)
                right = after - mid
                now = flux(i, mid, left, right)
                if flow is not None:
                    fresh = mid - now + flow
                    once[i] = fresh
                    if i - 1 in once:
                        right2 = fresh - once[i - 1]
                        if left2 is not None:
                            now2 = flux(i - 1, once[i - 1], left2, right2)
                            if flow2 is not None:
                                done.append(once[i - 1] - now2 + flow2)
                            flow2 = now2
                        left2 = right2
                flow, mid, left = now, after, right
            finished.append(done)
        for r in range(share_rows):
            both = jnp.concatenate([finished[c][r] for c in range(halves)], axis=1)
            spot = (r % per_group) * width
            send[d, r // per_group, :, spot : spot + width] = both.astype(BF16)

    def inner(d, carry):
        advect(d)
        return carry

    lax.fori_loop(1, n_spec - 1, inner, 0)

    pl.semaphore_wait(barrier, n_spec - 1 + len(steps))

    sides = [(rows - PAD, 0, up), (0, PAD + rows, down)]

    def send_halo(s, carry):
        for index, (origin, target, device) in enumerate(sides):
            for c in range(halves):
                pltpu.make_async_remote_copy(
                    conc.at[s, pl.ds(origin, PAD), pl.ds(c * BLK, BLK)],
                    field_in.at[index, c, pl.ds(pl.multiple_of(s * PAD, PAD), PAD), :],
                    halo_send.at[index], halo_recv.at[index], device_id={"tile": device}, device_id_type=MESH).start()
        return carry

    lax.fori_loop(0, species, send_halo, 0)
    halo = []
    for index, (origin, target, device) in enumerate(sides):
        whole = field_in.at[index]
        halo.append(pltpu.make_async_remote_copy(
            whole, whole, halo_send.at[index], halo_recv.at[index], device_id={"tile": device}, device_id_type=MESH))
        for c in range(halves):
            halo.append(pltpu.make_async_remote_copy(
                courant.at[pl.ds(origin, PAD), pl.ds(c * BLK, BLK)], rate_in.at[index, c],
                halo_send.at[2 + 2 * c + index], halo_recv.at[2 + 2 * c + index], device_id={"tile": device}, device_id_type=MESH))
            halo[-1].start()
    tallies = []
    for i, step in enumerate(steps):
        tallies.append(pltpu.make_async_remote_copy(
            counts.at[i + 1], counts_in.at[i], count_send.at[i], count_recv.at[i],
            device_id={"tile": (tile + step + n_tile) % n_tile}, device_id_type=MESH))
    for copy in tallies:
        copy.start()

    def message(d, g):
        return pltpu.make_async_remote_copy(
            send.at[d, g], recv.at[g, me], send_sem, recv_sem.at[g], device_id={"spec": d}, device_id_type=MESH)

    def first_group(k, carry):
        d = partner(k)

        @pl.when((d != 0) & (d != n_spec - 1))
        def _():
            message(d, 0).start()
        return carry

    lax.fori_loop(1, n_spec, first_group, 0)

    for copy in halo:
        copy.wait()
    for c in range(halves):
        for index, (_, target, _) in enumerate(sides):
            rate[c, target : target + PAD] = rate_in[index, c]
            for s in range(species):
                field[c, s * deep + target : s * deep + target + PAD] = field_in[index, c, s * PAD : (s + 1) * PAD]
            half_rest[c, target : target + PAD] = 0.5 * (1.0 - rate[c, target : target + PAD])

    def edge(e, carry):
        d = e * (n_spec - 1)
        advect(d)

        @pl.when(d != me)
        def _():
            message(d, 0).start()
        return carry

    lax.fori_loop(0, 2, edge, 0)

    def later(i, carry):
        g = i // (n_spec - 1)
        message(partner(i % (n_spec - 1) + 1), g).start()
        return carry

    lax.fori_loop(n_spec - 1, n_group * (n_spec - 1), later, 0)

    own = pltpu.make_async_copy(send.at[me], recv.at[:, me], own_sem)
    own.start()

    for copy in weights:
        copy.wait()
    w1_t[...] = (w1[...] * BF16(0.5)).T
    w2_t[...] = (w2[...] * BF16(0.5)).T
    own.wait()

    span = recv.shape[3]
    total = n_spec * species

    def integrate(g, carry):
        pltpu.make_async_remote_copy(
            recv.at[g, pl.ds(0, n_spec - 1)], recv.at[g, pl.ds(0, n_spec - 1)], send_sem, recv_sem.at[g],
            device_id={"spec": me}, device_id_type=MESH).wait_recv()
        x = recv[g].reshape(total, span)
        one = fused_silu(jnp.dot(w1_t[...], x, preferred_element_type=F32))
        two = fused_silu(jnp.dot(w2_t[...], one, preferred_element_type=F32))
        change = jnp.dot(w3_t[...], two, preferred_element_type=F32)
        fresh = (x.astype(F32) + change).astype(BF16)
        for b in range(span // BLK):
            block = g * (span // BLK) + b
            listed = jnp.int32(0)
            for j in range(active.shape[0]):
                listed = listed + jnp.where(active[j] == block, 1, 0)
            cols = slice(b * BLK, (b + 1) * BLK)
            chosen = jnp.where(jnp.full((total, BLK), listed, jnp.int32) > 0, fresh[:, cols].astype(F32), x[:, cols].astype(F32))
            out[:, pl.ds(pl.multiple_of(block * BLK, BLK), BLK)] = chosen.astype(BF16)
        return carry

    lax.fori_loop(0, n_group, integrate, 0)

    for copy in tallies:
        copy.wait()
    tally = counts[0] + counts_in[0] + counts_in[1] + counts_in[2] + counts_in[3]
    share[...] = tally[0:1, 0:1].astype(F32) / RECV

    pltpu.make_async_remote_copy(
        recv.at[:, pl.ds(0, n_spec - 1)], recv.at[:, pl.ds(0, n_spec - 1)], send_sem, own_sem,
        device_id={"spec": me}, device_id_type=MESH).wait_send()


def solution(mesh):
    n_tile, n_spec = mesh.shape["tile"], mesh.shape["spec"]

    def shards(conc, courant, w1, w2, w3, active, dest):
        species, rows, width = conc.shape
        hidden = w2.shape[0]
        halves = width // BLK
        total = n_spec * species
        cells = rows // n_spec * width
        span = cells // GROUPS
        deep = rows + 2 * PAD
        anywhere = pl.BlockSpec(memory_space=pl.ANY)
        scalars = pl.BlockSpec(memory_space=pltpu.SMEM)
        vector = pl.BlockSpec(memory_space=pltpu.VMEM)
        out, share = pl.pallas_call(
            functools.partial(kernel, n_tile, n_spec, 3, GROUPS),
            out_shape=(jax.ShapeDtypeStruct((total, cells), BF16), jax.ShapeDtypeStruct((1, 1), F32)),
            in_specs=[anywhere] * 5 + [scalars] * 2,
            out_specs=(vector, vector),
            scratch_shapes=[
                pltpu.VMEM((halves, species * deep, BLK), F32),
                pltpu.VMEM((halves, deep, BLK), F32),
                pltpu.VMEM((halves, deep, BLK), F32),
                pltpu.VMEM((2, halves, species * PAD, BLK), F32),
                pltpu.VMEM((2, halves, PAD, BLK), F32),
                pltpu.VMEM((n_spec, GROUPS, species, span), BF16),
                pltpu.VMEM((GROUPS, n_spec, species, span), BF16),
                pltpu.VMEM((total, hidden), BF16),
                pltpu.VMEM((hidden, hidden), BF16),
                pltpu.VMEM((hidden, total), BF16),
                pltpu.VMEM((hidden, hidden), BF16),
                pltpu.VMEM((total, hidden), BF16),
                pltpu.VMEM((5, 8, BLK), jnp.int32),
                pltpu.VMEM((4, 8, BLK), jnp.int32),
                pltpu.SemaphoreType.DMA((2 * halves,)),
                pltpu.SemaphoreType.DMA((3,)),
                pltpu.SemaphoreType.DMA((2 + 2 * halves,)),
                pltpu.SemaphoreType.DMA((2 + 2 * halves,)),
                pltpu.SemaphoreType.DMA((4,)),
                pltpu.SemaphoreType.DMA((4,)),
                pltpu.SemaphoreType.DMA,
                pltpu.SemaphoreType.DMA((GROUPS,)),
                pltpu.SemaphoreType.DMA,
            ],
            compiler_params=pltpu.CompilerParams(
                collective_id=0, has_side_effects=True, vmem_limit_bytes=60 * 1024 * 1024
            ),
            name="sweep_exchange_chemistry",
        )(conc, courant, w1, w2, w3.T, active.reshape(-1), dest.reshape(-1))
        return out, share

    in_specs = (
        P("spec", "tile", None),
        P("tile", None),
        P(),
        P(),
        P(),
        P("tile", "spec", None),
        P("tile", "spec", None),
    )
    out_specs = (P(None, ("tile", "spec")), P("tile", "spec"))
    return jax.shard_map(shards, mesh=mesh, in_specs=in_specs, out_specs=out_specs, check_vma=False)
```

time: 151 us -> 81 us (0.54)
  the two profiles are of different devices: /device:TPU:167 before, /device:TPU:1 now
where the time goes in v1:
time: 81 us; the launch traced here: 80 us
  Pallas kernels  74.9 us (92%)
  local copies, waits for them, and re-layouts  2.7 us (3%)
  between operations  2.41 us (3%)
    pallas_call x1, Pallas kernels, shards(): pl.pallas_call(functools.partial(kernel, n_tile, n_spec, 3, GROUPS), out_...  74.9 us
    unnamed x1, local copies, waits for them, and re-layouts  2.7 us

profile of v1, /device:TPU:1, one launch (start us, length us, event | category | flops | bytes accessed | tf_op | source)
XLA Modules:
  0.0 80.0 jit_solution(8783788282543174447)
XLA Ops:
  0.6 74.9 %sweep_exchange_chemistry.1 = (bf16[192,4096]{1,0:T(8,128)(2,1)}, f32[1,1]{1,0:T(1,128)}) custom-call(f32[8,384,256]{2,1,0:T(8,128)} %conc.1, f32[384,256]{1,0:T(8,128)} %courant.1, bf16[192,512]{1,0:T(8,128)(2,1)} %w1_hbm.1, bf16[512,512]{1,0:T(8,128)(2,1)} %w2_hbm.1, bf16[192,512]{1,0:T(8,128)(2,1)} %bitcast.3, s32[16]{0:T(128)} %bitcast.4, s32[16]{0:T(128)} %bitcast.5), custom_call_target="tpu_custom_call" | custom-call | tf_op jit(solution)/shard_map/sweep_exchange_chemistry/pallas_call | solution.py:277
  75.5 2.7 %copy.11 = bf16[192,4096]{1,0:T(8,128)(2,1)} copy(bf16[192,4096]{1,0:T(8,128)(2,1)} %get-tuple-element.4) | data formatting | bytes 3145728

commit v2 on v1

--- a/solution.py
+++ b/solution.py
@@ -29,8 +29,8 @@
     n_tile, n_spec, n_z, n_group,
     conc, courant, w1_hbm, w2_hbm, w3_hbm, active, dest,
     out, share,
-    field, rate, half_rest, field_in, rate_in, send, recv, w1, w2, w1_t, w2_t, w3_t, counts, counts_in,
-    load_sem, weight_sem, halo_send, halo_recv, count_send, count_recv, send_sem, recv_sem, own_sem,
+    field, rate, half_rest, field_out, field_in, rate_in, send, recv, w1, w2, w1_t, w2_t, w3_t, counts, counts_in,
+    load_sem, weight_sem, halo_send, halo_recv, count_send, count_recv, send_sem, recv_sem, own_sem, known,
 ):
     tile = lax.axis_index("tile")
     me = lax.axis_index("spec")
@@ -74,12 +74,15 @@
 
     barrier = pltpu.get_barrier_semaphore()
 
-    def greet(k, carry):
-        pl.semaphore_signal(barrier, inc=1, device_id={"spec": partner(k)}, device_id_type=MESH)
-        return carry
-
-    lax.fori_loop(1, n_spec, greet, 0)
+    def at(dy, dz):
+        return ((my_y + dy + n_y) % n_y) * n_z + (my_z + dz) % n_z
+
     steps = [1, -1, 2, -2]
+    column = list(range(1, n_z))
+    for dz in column:
+        pl.semaphore_signal(barrier, inc=1, device_id={"spec": at(0, dz)}, device_id_type=MESH)
+    for dy in (1, -1):
+        pl.semaphore_signal(barrier, inc=1, device_id={"spec": at(dy, 0)}, device_id_type=MESH)
     for step in steps:
         pl.semaphore_signal(barrier, inc=1, device_id={"tile": (tile + step + n_tile) % n_tile}, device_id_type=MESH)
 
@@ -96,6 +99,12 @@
         copy.wait()
     for c in range(halves):
         half_rest[c, PAD : PAD + rows] = 0.5 * (1.0 - rate[c, PAD : PAD + rows])
+
+    sides = [(PAD + rows - 4, 4, 4, up), (PAD, PAD + rows, 2, down)]
+    for index, (origin, _, thick, _) in enumerate(sides):
+        for c in range(halves):
+            for s in range(species):
+                field_out[index, c, s * thick : (s + 1) * thick] = field[c, s * deep + origin : s * deep + origin + thick]
 
     def advect(d):
         first = PAD + d * share_rows
@@ -144,30 +153,35 @@
 
     lax.fori_loop(1, n_spec - 1, inner, 0)
 
-    pl.semaphore_wait(barrier, n_spec - 1 + len(steps))
-
-    sides = [(rows - PAD, 0, up), (0, PAD + rows, down)]
-
-    def send_halo(s, carry):
-        for index, (origin, target, device) in enumerate(sides):
-            for c in range(halves):
-                pltpu.make_async_remote_copy(
-                    conc.at[s, pl.ds(origin, PAD), pl.ds(c * BLK, BLK)],
-                    field_in.at[index, c, pl.ds(pl.multiple_of(s * PAD, PAD), PAD), :],
-                    halo_send.at[index], halo_recv.at[index], device_id={"tile": device}, device_id_type=MESH).start()
-        return carry
-
-    lax.fori_loop(0, species, send_halo, 0)
+    pl.semaphore_wait(barrier, len(column) + 2 + len(steps))
+
+    def message(d, g):
+        return pltpu.make_async_remote_copy(
+            send.at[d, g], recv.at[g, me], send_sem, recv_sem.at[g], device_id={"spec": d}, device_id_type=MESH)
+
+    def inside(d):
+        return (d != 0) & (d != n_spec - 1)
+
+    for dz in column:
+        @pl.when(inside(at(0, dz)))
+        def _(d=at(0, dz)):
+            def every(g, carry):
+                message(d, g).start()
+                return carry
+
+            lax.fori_loop(0, n_group, every, 0)
+
     halo = []
-    for index, (origin, target, device) in enumerate(sides):
-        whole = field_in.at[index]
-        halo.append(pltpu.make_async_remote_copy(
-            whole, whole, halo_send.at[index], halo_recv.at[index], device_id={"tile": device}, device_id_type=MESH))
+    for index, (_, _, thick, device) in enumerate(sides):
         for c in range(halves):
             halo.append(pltpu.make_async_remote_copy(
-                courant.at[pl.ds(origin, PAD), pl.ds(c * BLK, BLK)], rate_in.at[index, c],
-                halo_send.at[2 + 2 * c + index], halo_recv.at[2 + 2 * c + index], device_id={"tile": device}, device_id_type=MESH))
-            halo[-1].start()
+                field_out.at[index, c, pl.ds(0, species * thick)], field_in.at[index, c, pl.ds(0, species * thick)],
+                halo_send.at[2 * c + index], halo_recv.at[2 * c + index], device_id={"tile": device}, device_id_type=MESH))
+            halo.append(pltpu.make_async_remote_copy(
+                rate.at[c, pl.ds(PAD + (rows - PAD if index == 0 else 0), PAD), :], rate_in.at[index, c],
+                halo_send.at[4 + 2 * c + index], halo_recv.at[4 + 2 * c + index], device_id={"tile": device}, device_id_type=MESH))
+    for copy in halo:
+        copy.start()
     tallies = []
     for i, step in enumerate(steps):
         tallies.append(pltpu.make_async_remote_copy(
@@ -176,28 +190,26 @@
     for copy in tallies:
         copy.start()
 
-    def message(d, g):
-        return pltpu.make_async_remote_copy(
-            send.at[d, g], recv.at[g, me], send_sem, recv_sem.at[g], device_id={"spec": d}, device_id_type=MESH)
-
-    def first_group(k, carry):
-        d = partner(k)
-
-        @pl.when((d != 0) & (d != n_spec - 1))
-        def _():
-            message(d, 0).start()
-        return carry
-
-    lax.fori_loop(1, n_spec, first_group, 0)
+    for reach in range(1, n_y // 2 + 1):
+        for way, dy in enumerate((1, -1)):
+            pl.semaphore_signal(known.at[reach - 1, way], inc=1, device_id={"spec": at(dy, 0)}, device_id_type=MESH)
+        for way in range(2):
+            pl.semaphore_wait(known.at[reach - 1, way], 1)
+        for dy in sorted({reach, n_y - reach}):
+            for dz in column + [0]:
+                @pl.when(inside(at(dy, dz)))
+                def _(d=at(dy, dz)):
+                    message(d, 0).start()
 
     for copy in halo:
         copy.wait()
     for c in range(halves):
-        for index, (_, target, _) in enumerate(sides):
-            rate[c, target : target + PAD] = rate_in[index, c]
+        for index, (_, target, thick, _) in enumerate(sides):
+            base = index * (PAD + rows)
+            rate[c, base : base + PAD] = rate_in[index, c]
             for s in range(species):
-                field[c, s * deep + target : s * deep + target + PAD] = field_in[index, c, s * PAD : (s + 1) * PAD]
-            half_rest[c, target : target + PAD] = 0.5 * (1.0 - rate[c, target : target + PAD])
+                field[c, s * deep + target : s * deep + target + thick] = field_in[index, c, s * thick : (s + 1) * thick]
+            half_rest[c, base : base + PAD] = 0.5 * (1.0 - rate[c, base : base + PAD])
 
     def edge(e, carry):
         d = e * (n_spec - 1)
@@ -211,8 +223,12 @@
     lax.fori_loop(0, 2, edge, 0)
 
     def later(i, carry):
-        g = i // (n_spec - 1)
-        message(partner(i % (n_spec - 1) + 1), g).start()
+        g, k = i // (n_spec - 1), i % (n_spec - 1) + 1
+        d = partner(k)
+
+        @pl.when((k % n_y != 0) | (d == 0) | (d == n_spec - 1))
+        def _():
+            message(d, g).start()
         return carry
 
     lax.fori_loop(n_spec - 1, n_group * (n_spec - 1), later, 0)
@@ -276,14 +292,15 @@
         vector = pl.BlockSpec(memory_space=pltpu.VMEM)
         out, share = pl.pallas_call(
             functools.partial(kernel, n_tile, n_spec, 3, GROUPS),
-            out_shape=(jax.ShapeDtypeStruct((total, cells), BF16), jax.ShapeDtypeStruct((1, 1), F32)),
+            out_shape=(pltpu.VMEM((total, cells), BF16), jax.ShapeDtypeStruct((1, 1), F32)),
             in_specs=[anywhere] * 5 + [scalars] * 2,
             out_specs=(vector, vector),
             scratch_shapes=[
                 pltpu.VMEM((halves, species * deep, BLK), F32),
                 pltpu.VMEM((halves, deep, BLK), F32),
                 pltpu.VMEM((halves, deep, BLK), F32),
-                pltpu.VMEM((2, halves, species * PAD, BLK), F32),
+                pltpu.VMEM((2, halves, species * 4, BLK), F32),
+                pltpu.VMEM((2, halves, species * 4, BLK), F32),
                 pltpu.VMEM((2, halves, PAD, BLK), F32),
                 pltpu.VMEM((n_spec, GROUPS, species, span), BF16),
                 pltpu.VMEM((GROUPS, n_spec, species, span), BF16),
@@ -296,13 +313,14 @@
                 pltpu.VMEM((4, 8, BLK), jnp.int32),
                 pltpu.SemaphoreType.DMA((2 * halves,)),
                 pltpu.SemaphoreType.DMA((3,)),
-                pltpu.SemaphoreType.DMA((2 + 2 * halves,)),
-                pltpu.SemaphoreType.DMA((2 + 2 * halves,)),
+                pltpu.SemaphoreType.DMA((4 * halves,)),
+                pltpu.SemaphoreType.DMA((4 * halves,)),
                 pltpu.SemaphoreType.DMA((4,)),
                 pltpu.SemaphoreType.DMA((4,)),
                 pltpu.SemaphoreType.DMA,
                 pltpu.SemaphoreType.DMA((GROUPS,)),
                 pltpu.SemaphoreType.DMA,
+                pltpu.SemaphoreType.REGULAR((max(n_spec // 6, 1), 2)),
             ],
             compiler_params=pltpu.CompilerParams(
                 collective_id=0, has_side_effects=True, vmem_limit_bytes=60 * 1024 * 1024

time: 81 us -> 79.1 us (0.977)
  the two profiles are of different devices: /device:TPU:1 before, /device:TPU:192 now
where the time goes in v2:
time: 79.1 us; the launch traced here: 79 us
  Pallas kernels  75.5 us (95%)
  between operations  2.33 us (3%)
  local copies, waits for them, and re-layouts  1.15 us (1%)
    pallas_call x1, Pallas kernels, shards(): pl.pallas_call(functools.partial(kernel, n_tile, n_spec, 3, GROUPS), out_...  75.5 us

profile of v2, /device:TPU:192, one launch (start us, length us, event | category | flops | bytes accessed | tf_op | source)
XLA Modules:
  0.0 79.0 jit_solution(15510204074147998680)
XLA Ops:
  0.6 75.5 %sweep_exchange_chemistry.1 = (bf16[192,4096]{1,0:T(8,128)(2,1)S(1)}, f32[1,1]{1,0:T(1,128)}) custom-call(f32[8,384,256]{2,1,0:T(8,128)} %conc.1, f32[384,256]{1,0:T(8,128)} %courant.1, bf16[192,512]{1,0:T(8,128)(2,1)} %w1_hbm.1, bf16[512,512]{1,0:T(8,128)(2,1)} %w2_hbm.1, bf16[192,512]{1,0:T(8,128)(2,1)} %bitcast.3, s32[16]{0:T(128)} %bitcast.4, s32[16]{0:T(128)} %bitcast.5), custom_call_target="tpu_custom_call" | custom-call | tf_op jit(solution)/shard_map/sweep_exchange_chemistry/pallas_call | solution.py:293
  76.1 1.1 %copy.11 = bf16[192,4096]{1,0:T(8,128)(2,1)} copy(bf16[192,4096]{1,0:T(8,128)(2,1)S(1)} %get-tuple-element.2) | data formatting | bytes 3145728

commit v3 on v2

--- a/solution.py
+++ b/solution.py
@@ -147,20 +147,22 @@
             spot = (r % per_group) * width
             send[d, r // per_group, :, spot : spot + width] = both.astype(BF16)
 
-    def inner(d, carry):
-        advect(d)
-        return carry
-
-    lax.fori_loop(1, n_spec - 1, inner, 0)
+    def inside(d):
+        return (d != 0) & (d != n_spec - 1)
+
+    def first(dz, carry):
+        @pl.when(inside(at(0, dz)))
+        def _():
+            advect(at(0, dz))
+        return carry
+
+    lax.fori_loop(1, n_z, first, 0)
 
     pl.semaphore_wait(barrier, len(column) + 2 + len(steps))
 
     def message(d, g):
         return pltpu.make_async_remote_copy(
             send.at[d, g], recv.at[g, me], send_sem, recv_sem.at[g], device_id={"spec": d}, device_id_type=MESH)
-
-    def inside(d):
-        return (d != 0) & (d != n_spec - 1)
 
     for dz in column:
         @pl.when(inside(at(0, dz)))
@@ -190,16 +192,38 @@
     for copy in tallies:
         copy.start()
 
-    for reach in range(1, n_y // 2 + 1):
+    farthest = n_y // 2
+
+    def stage(reach, carry):
         for way, dy in enumerate((1, -1)):
             pl.semaphore_signal(known.at[reach - 1, way], inc=1, device_id={"spec": at(dy, 0)}, device_id_type=MESH)
+
+        def piece(i):
+            return at(jnp.where(i < n_z, reach, -reach), i + 1)
+
+        def sweep(i, carry):
+            alone = (reach == farthest) & (i == n_z)
+            d = jnp.where(alone, me, piece(i))
+
+            @pl.when(inside(d) & ((reach < farthest) | (i <= n_z)))
+            def _():
+                advect(d)
+            return carry
+
+        lax.fori_loop(0, 2 * n_z, sweep, 0)
         for way in range(2):
             pl.semaphore_wait(known.at[reach - 1, way], 1)
-        for dy in sorted({reach, n_y - reach}):
-            for dz in column + [0]:
-                @pl.when(inside(at(dy, dz)))
-                def _(d=at(dy, dz)):
-                    message(d, 0).start()
+
+        def post(i, carry):
+            @pl.when(inside(piece(i)) & ((reach < farthest) | (i < n_z)))
+            def _():
+                message(piece(i), 0).start()
+            return carry
+
+        lax.fori_loop(0, 2 * n_z, post, 0)
+        return carry
+
+    lax.fori_loop(1, farthest + 1, stage, 0)
 
     for copy in halo:
         copy.wait()

time: 79.1 us -> 76.8 us (0.971)
  the two profiles are of different devices: /device:TPU:192 before, /device:TPU:1 now
where the time goes in v3:
time: 76.8 us; the launch traced here: 76.6 us
  Pallas kernels  73.1 us (95%)
  between operations  2.33 us (3%)
  local copies, waits for them, and re-layouts  1.15 us (1%)
    pallas_call x1, Pallas kernels, shards(): pl.pallas_call(functools.partial(kernel, n_tile, n_spec, 3, GROUPS), out_...  73.1 us

profile of v3, /device:TPU:1, one launch (start us, length us, event | category | flops | bytes accessed | tf_op | source)
XLA Modules:
  0.0 76.6 jit_solution(3849858137996181420)
XLA Ops:
  0.6 73.1 %sweep_exchange_chemistry.1 = (bf16[192,4096]{1,0:T(8,128)(2,1)S(1)}, f32[1,1]{1,0:T(1,128)}) custom-call(f32[8,384,256]{2,1,0:T(8,128)} %conc.1, f32[384,256]{1,0:T(8,128)} %courant.1, bf16[192,512]{1,0:T(8,128)(2,1)} %w1_hbm.1, bf16[512,512]{1,0:T(8,128)(2,1)} %w2_hbm.1, bf16[192,512]{1,0:T(8,128)(2,1)} %bitcast.3, s32[16]{0:T(128)} %bitcast.4, s32[16]{0:T(128)} %bitcast.5), custom_call_target="tpu_custom_call" | custom-call | tf_op jit(solution)/shard_map/sweep_exchange_chemistry/pallas_call | solution.py:317
  73.7 1.1 %copy.11 = bf16[192,4096]{1,0:T(8,128)(2,1)} copy(bf16[192,4096]{1,0:T(8,128)(2,1)S(1)} %get-tuple-element.2) | data formatting | bytes 3145728

commit v4 on v3

--- a/solution.py
+++ b/solution.py
@@ -27,9 +27,9 @@
 
 def kernel(
     n_tile, n_spec, n_z, n_group,
-    conc, courant, w1_hbm, w2_hbm, w3_hbm, active, dest,
+    conc, courant, w1_hbm, w2_hbm, w3_hbm, active_hbm, dest_hbm,
     out, share,
-    field, rate, half_rest, field_out, field_in, rate_in, send, recv, w1, w2, w1_t, w2_t, w3_t, counts, counts_in,
+    field, rate, half_rest, field_out, field_in, rate_in, send, recv, w1, w2, w1_t, w2_t, w3_t, counts, counts_in, active, dest,
     load_sem, weight_sem, halo_send, halo_recv, count_send, count_recv, send_sem, recv_sem, own_sem, known,
 ):
     tile = lax.axis_index("tile")
@@ -47,6 +47,20 @@
     def partner(k):
         return ((my_y + k) % n_y) * n_z + (my_z + k) % n_z
 
+    barrier = pltpu.get_barrier_semaphore()
+
+    def at(dy, dz):
+        return ((my_y + dy + n_y) % n_y) * n_z + (my_z + dz) % n_z
+
+    steps = [1, -1, 2, -2]
+    column = list(range(1, n_z))
+    for dz in column:
+        pl.semaphore_signal(barrier, inc=1, device_id={"spec": at(0, dz)}, device_id_type=MESH)
+    for dy in (1, -1):
+        pl.semaphore_signal(barrier, inc=1, device_id={"spec": at(dy, 0)}, device_id_type=MESH)
+    for step in steps:
+        pl.semaphore_signal(barrier, inc=1, device_id={"tile": (tile + step + n_tile) % n_tile}, device_id_type=MESH)
+
     species = conc.shape[0]
 
     def load(s, carry):
@@ -69,31 +83,12 @@
         pltpu.make_async_copy(w2_hbm, w2, weight_sem.at[1]),
         pltpu.make_async_copy(w3_hbm, w3_t, weight_sem.at[2]),
     ]
-    for copy in weights:
+    lists = [
+        pltpu.make_async_copy(active_hbm, active, weight_sem.at[3]),
+        pltpu.make_async_copy(dest_hbm, dest, weight_sem.at[4]),
+    ]
+    for copy in lists + weights:
         copy.start()
-
-    barrier = pltpu.get_barrier_semaphore()
-
-    def at(dy, dz):
-        return ((my_y + dy + n_y) % n_y) * n_z + (my_z + dz) % n_z
-
-    steps = [1, -1, 2, -2]
-    column = list(range(1, n_z))
-    for dz in column:
-        pl.semaphore_signal(barrier, inc=1, device_id={"spec": at(0, dz)}, device_id_type=MESH)
-    for dy in (1, -1):
-        pl.semaphore_signal(barrier, inc=1, device_id={"spec": at(dy, 0)}, device_id_type=MESH)
-    for step in steps:
-        pl.semaphore_signal(barrier, inc=1, device_id={"tile": (tile + step + n_tile) % n_tile}, device_id_type=MESH)
-
-    named = [jnp.int32(0)] * 5
-    for j in range(active.shape[0]):
-        home = (dest[j] - tile + n_tile + n_tile // 2) % n_tile - n_tile // 2
-        valid = active[j] < out.shape[1] // BLK
-        for i, step in enumerate([0] + steps):
-            named[i] = named[i] + jnp.where(valid & (home == step), 1, 0)
-    for i in range(5):
-        counts[i] = jnp.full(counts.shape[1:], named[i], jnp.int32)
 
     for copy in loads:
         copy.wait()
@@ -184,6 +179,17 @@
                 halo_send.at[4 + 2 * c + index], halo_recv.at[4 + 2 * c + index], device_id={"tile": device}, device_id_type=MESH))
     for copy in halo:
         copy.start()
+    for copy in lists:
+        copy.wait()
+    named = [jnp.int32(0)] * 5
+    for j in range(active.shape[0]):
+        home = (dest[j] - tile + n_tile + n_tile // 2) % n_tile - n_tile // 2
+        valid = active[j] < out.shape[1] // BLK
+        for i, step in enumerate([0] + steps):
+            named[i] = named[i] + jnp.where(valid & (home == step), 1, 0)
+    for i in range(5):
+        counts[i] = jnp.full(counts.shape[1:], named[i], jnp.int32)
+
     tallies = []
     for i, step in enumerate(steps):
         tallies.append(pltpu.make_async_remote_copy(
@@ -312,12 +318,11 @@
         span = cells // GROUPS
         deep = rows + 2 * PAD
         anywhere = pl.BlockSpec(memory_space=pl.ANY)
-        scalars = pl.BlockSpec(memory_space=pltpu.SMEM)
         vector = pl.BlockSpec(memory_space=pltpu.VMEM)
         out, share = pl.pallas_call(
             functools.partial(kernel, n_tile, n_spec, 3, GROUPS),
-            out_shape=(pltpu.VMEM((total, cells), BF16), jax.ShapeDtypeStruct((1, 1), F32)),
-            in_specs=[anywhere] * 5 + [scalars] * 2,
+            out_shape=(pltpu.VMEM((total, cells), BF16), pltpu.VMEM((1, 1), F32)),
+            in_specs=[anywhere] * 7,
             out_specs=(vector, vector),
             scratch_shapes=[
                 pltpu.VMEM((halves, species * deep, BLK), F32),
@@ -335,8 +340,10 @@
                 pltpu.VMEM((total, hidden), BF16),
                 pltpu.VMEM((5, 8, BLK), jnp.int32),
                 pltpu.VMEM((4, 8, BLK), jnp.int32),
+                pltpu.SMEM((active.size,), jnp.int32),
+                pltpu.SMEM((dest.size,), jnp.int32),
                 pltpu.SemaphoreType.DMA((2 * halves,)),
-                pltpu.SemaphoreType.DMA((3,)),
+                pltpu.SemaphoreType.DMA((5,)),
                 pltpu.SemaphoreType.DMA((4 * halves,)),
                 pltpu.SemaphoreType.DMA((4 * halves,)),
                 pltpu.SemaphoreType.DMA((4,)),

time: 76.8 us -> 74.7 us (0.973)
  the two profiles are of different devices: /device:TPU:1 before, /device:TPU:64 now
where the time goes in v4:
time: 74.7 us; the launch traced here: 74.5 us
  Pallas kernels  72.2 us (97%)
  between operations  1.18 us (2%)
  local copies, waits for them, and re-layouts  1.14 us (2%)
    pallas_call x1, Pallas kernels, shards(): pl.pallas_call(functools.partial(kernel, n_tile, n_spec, 3, GROUPS), out_...  72.2 us

profile of v4, /device:TPU:64, one launch (start us, length us, event | category | flops | bytes accessed | tf_op | source)
XLA Modules:
  0.0 74.5 jit_solution(16852191032439611029)
XLA Ops:
  0.6 72.2 %sweep_exchange_chemistry.1 = (bf16[192,4096]{1,0:T(8,128)(2,1)S(1)}, f32[1,1]{1,0:T(1,128)S(1)}) custom-call(f32[8,384,256]{2,1,0:T(8,128)} %conc.1, f32[384,256]{1,0:T(8,128)} %courant.1, bf16[192,512]{1,0:T(8,128)(2,1)} %w1_hbm.1, bf16[512,512]{1,0:T(8,128)(2,1)} %w2_hbm.1, bf16[192,512]{1,0:T(8,128)(2,1)} %bitcast.3, s32[16]{0:T(128)} %bitcast.4, s32[16]{0:T(128)} %bitcast.5), custom_call_target="tpu_custom_call" | custom-call | tf_op jit(solution)/shard_map/sweep_exchange_chemistry/pallas_call | solution.py:322
  73.4 1.1 %copy.11 = bf16[192,4096]{1,0:T(8,128)(2,1)} copy(bf16[192,4096]{1,0:T(8,128)(2,1)S(1)} %get-tuple-element.2) | data formatting | bytes 3145728

commit v5 on v4

--- a/solution.py
+++ b/solution.py
@@ -87,8 +87,6 @@
         pltpu.make_async_copy(active_hbm, active, weight_sem.at[3]),
         pltpu.make_async_copy(dest_hbm, dest, weight_sem.at[4]),
     ]
-    for copy in lists + weights:
-        copy.start()
 
     for copy in loads:
         copy.wait()
@@ -96,11 +94,6 @@
         half_rest[c, PAD : PAD + rows] = 0.5 * (1.0 - rate[c, PAD : PAD + rows])
 
     sides = [(PAD + rows - 4, 4, 4, up), (PAD, PAD + rows, 2, down)]
-    for index, (origin, _, thick, _) in enumerate(sides):
-        for c in range(halves):
-            for s in range(species):
-                field_out[index, c, s * thick : (s + 1) * thick] = field[c, s * deep + origin : s * deep + origin + thick]
-
     def advect(d):
         first = PAD + d * share_rows
         finished = []
@@ -167,6 +160,13 @@
                 return carry
 
             lax.fori_loop(0, n_group, every, 0)
+
+    for copy in lists + weights:
+        copy.start()
+    for index, (origin, _, thick, _) in enumerate(sides):
+        for c in range(halves):
+            for s in range(species):
+                field_out[index, c, s * thick : (s + 1) * thick] = field[c, s * deep + origin : s * deep + origin + thick]
 
     halo = []
     for index, (_, _, thick, device) in enumerate(sides):

time: 74.7 us -> 74.4 us (level)
  the two profiles are of different devices: /device:TPU:64 before, /device:TPU:1 now
where the time goes in v5:
time: 74.4 us; the launch traced here: 74.2 us
  Pallas kernels  71.9 us (97%)
  between operations  1.18 us (2%)
  local copies, waits for them, and re-layouts  1.14 us (2%)
    pallas_call x1, Pallas kernels, shards(): pl.pallas_call(functools.partial(kernel, n_tile, n_spec, 3, GROUPS), out_...  71.9 us

profile of v5, /device:TPU:1, one launch (start us, length us, event | category | flops | bytes accessed | tf_op | source)
XLA Modules:
  0.0 74.2 jit_solution(12730324844041338936)
XLA Ops:
  0.6 71.9 %sweep_exchange_chemistry.1 = (bf16[192,4096]{1,0:T(8,128)(2,1)S(1)}, f32[1,1]{1,0:T(1,128)S(1)}) custom-call(f32[8,384,256]{2,1,0:T(8,128)} %conc.1, f32[384,256]{1,0:T(8,128)} %courant.1, bf16[192,512]{1,0:T(8,128)(2,1)} %w1_hbm.1, bf16[512,512]{1,0:T(8,128)(2,1)} %w2_hbm.1, bf16[192,512]{1,0:T(8,128)(2,1)} %bitcast.3, s32[16]{0:T(128)} %bitcast.4, s32[16]{0:T(128)} %bitcast.5), custom_call_target="tpu_custom_call" | custom-call | tf_op jit(solution)/shard_map/sweep_exchange_chemistry/pallas_call | solution.py:322
  73.1 1.1 %copy.11 = bf16[192,4096]{1,0:T(8,128)(2,1)} copy(bf16[192,4096]{1,0:T(8,128)(2,1)S(1)} %get-tuple-element.2) | data formatting | bytes 3145728

commit v6 on v5

--- a/solution.py
+++ b/solution.py
@@ -25,11 +25,23 @@
     return (half + half * jnp.tanh(half)).astype(BF16)
 
 
+def chemistry(x, w1_t, w2_t, w3_t):
+    one = fused_silu(jnp.dot(w1_t[...], x, preferred_element_type=F32))
+    two = fused_silu(jnp.dot(w2_t[...], one, preferred_element_type=F32))
+    change = jnp.dot(w3_t[...], two, preferred_element_type=F32)
+    return (x.astype(F32) + change).astype(BF16)
+
+
+def choose(flag, fresh, kept):
+    mask = jnp.tile(flag, (fresh.shape[0] // flag.shape[0], 1)) > 0
+    return jnp.where(mask, fresh.astype(F32), kept.astype(F32)).astype(BF16)
+
+
 def kernel(
     n_tile, n_spec, n_z, n_group,
     conc, courant, w1_hbm, w2_hbm, w3_hbm, active_hbm, dest_hbm,
-    out, share,
-    field, rate, half_rest, field_out, field_in, rate_in, send, recv, w1, w2, w1_t, w2_t, w3_t, counts, counts_in, active, dest,
+    out, share, w1_t, w2_t, w3_t, flags,
+    field, rate, half_rest, field_out, field_in, rate_in, send, recv, w1, w2, counts, counts_in, active, dest,
     load_sem, weight_sem, halo_send, halo_recv, count_send, count_recv, send_sem, recv_sem, own_sem, known,
 ):
     tile = lax.axis_index("tile")
@@ -275,35 +287,57 @@
     span = recv.shape[3]
     total = n_spec * species
 
-    def integrate(g, carry):
+    def arrived(g):
         pltpu.make_async_remote_copy(
             recv.at[g, pl.ds(0, n_spec - 1)], recv.at[g, pl.ds(0, n_spec - 1)], send_sem, recv_sem.at[g],
             device_id={"spec": me}, device_id_type=MESH).wait_recv()
+
+    def listed(block):
+        hits = jnp.int32(0)
+        for j in range(active.shape[0]):
+            hits = hits + jnp.where(active[j] == block, 1, 0)
+        return jnp.full((8, BLK), hits, jnp.int32)
+
+    def integrate(g, carry):
+        arrived(g)
         x = recv[g].reshape(total, span)
-        one = fused_silu(jnp.dot(w1_t[...], x, preferred_element_type=F32))
-        two = fused_silu(jnp.dot(w2_t[...], one, preferred_element_type=F32))
-        change = jnp.dot(w3_t[...], two, preferred_element_type=F32)
-        fresh = (x.astype(F32) + change).astype(BF16)
+        fresh = chemistry(x, w1_t, w2_t, w3_t)
         for b in range(span // BLK):
             block = g * (span // BLK) + b
-            listed = jnp.int32(0)
-            for j in range(active.shape[0]):
-                listed = listed + jnp.where(active[j] == block, 1, 0)
             cols = slice(b * BLK, (b + 1) * BLK)
-            chosen = jnp.where(jnp.full((total, BLK), listed, jnp.int32) > 0, fresh[:, cols].astype(F32), x[:, cols].astype(F32))
-            out[:, pl.ds(pl.multiple_of(block * BLK, BLK), BLK)] = chosen.astype(BF16)
-        return carry
-
-    lax.fori_loop(0, n_group, integrate, 0)
+            out[:, pl.ds(pl.multiple_of(block * BLK, BLK), BLK)] = choose(listed(block), fresh[:, cols], x[:, cols])
+        return carry
+
+    lax.fori_loop(0, n_group - 1, integrate, 0)
+    for b in range(span // BLK):
+        flags[b] = listed((n_group - 1) * (span // BLK) + b)
 
     for copy in tallies:
         copy.wait()
     tally = counts[0] + counts_in[0] + counts_in[1] + counts_in[2] + counts_in[3]
     share[...] = tally[0:1, 0:1].astype(F32) / RECV
 
+    arrived(n_group - 1)
+    out[:, (n_group - 1) * span :] = recv[n_group - 1].reshape(total, span)
     pltpu.make_async_remote_copy(
         recv.at[:, pl.ds(0, n_spec - 1)], recv.at[:, pl.ds(0, n_spec - 1)], send_sem, own_sem,
         device_id={"spec": me}, device_id_type=MESH).wait_send()
+
+
+def finish(part, w1_t, w2_t, w3_t, flags, out, last, sems):
+    total, span = last.shape
+    head = part.shape[1] - span
+    done = pltpu.make_async_copy(part.at[:, pl.ds(0, head)], out.at[:, pl.ds(0, head)], sems.at[0])
+    done.start()
+    x = part[:, head:]
+    fresh = chemistry(x, w1_t, w2_t, w3_t)
+    for b in range(span // BLK):
+        cols = slice(b * BLK, (b + 1) * BLK)
+        last[:, cols] = choose(flags[b], fresh[:, cols], x[:, cols])
+    tail = pltpu.make_async_copy(last, out.at[:, pl.ds(head, span)], sems.at[1])
+    tail.start()
+    done.wait()
+    tail.wait()
 
 
 def solution(mesh):
@@ -319,11 +353,18 @@
         deep = rows + 2 * PAD
         anywhere = pl.BlockSpec(memory_space=pl.ANY)
         vector = pl.BlockSpec(memory_space=pltpu.VMEM)
-        out, share = pl.pallas_call(
+        part, share, *rest = pl.pallas_call(
             functools.partial(kernel, n_tile, n_spec, 3, GROUPS),
-            out_shape=(pltpu.VMEM((total, cells), BF16), pltpu.VMEM((1, 1), F32)),
+            out_shape=(
+                pltpu.VMEM((total, cells), BF16),
+                pltpu.VMEM((1, 1), F32),
+                pltpu.VMEM((hidden, total), BF16),
+                pltpu.VMEM((hidden, hidden), BF16),
+                pltpu.VMEM((total, hidden), BF16),
+                pltpu.VMEM((span // BLK, 8, BLK), jnp.int32),
+            ),
             in_specs=[anywhere] * 7,
-            out_specs=(vector, vector),
+            out_specs=(vector,) * 6,
             scratch_shapes=[
                 pltpu.VMEM((halves, species * deep, BLK), F32),
                 pltpu.VMEM((halves, deep, BLK), F32),
@@ -335,9 +376,6 @@
                 pltpu.VMEM((GROUPS, n_spec, species, span), BF16),
                 pltpu.VMEM((total, hidden), BF16),
                 pltpu.VMEM((hidden, hidden), BF16),
-                pltpu.VMEM((hidden, total), BF16),
-                pltpu.VMEM((hidden, hidden), BF16),
-                pltpu.VMEM((total, hidden), BF16),
                 pltpu.VMEM((5, 8, BLK), jnp.int32),
                 pltpu.VMEM((4, 8, BLK), jnp.int32),
                 pltpu.SMEM((active.size,), jnp.int32),
@@ -358,6 +396,15 @@
             ),
             name="sweep_exchange_chemistry",
         )(conc, courant, w1, w2, w3.T, active.reshape(-1), dest.reshape(-1))
+        out = pl.pallas_call(
+            finish,
+            out_shape=jax.ShapeDtypeStruct((total, cells), BF16),
+            in_specs=[vector] * 5,
+            out_specs=anywhere,
+            scratch_shapes=[pltpu.VMEM((total, span), BF16), pltpu.SemaphoreType.DMA((2,))],
+            compiler_params=pltpu.CompilerParams(vmem_limit_bytes=24 * 1024 * 1024),
+            name="last_group",
+        )(*[pltpu.with_memory_space_constraint(a, pltpu.VMEM) for a in (part, *rest)])
         return out, share
 
     in_specs = (

time: 74.4 us -> 73.9 us (level)
  local copies, waits for them, and re-layouts: 1.14 us -> 0 us
    pallas_call x0 -> x1, Pallas kernels: none -> 1.54 us  [shards(): pl.pallas_call(finish, out_shape=jax.ShapeDtypeStruct((total, cells), BF1...]
    unnamed x1 -> x0, local copies, waits for them, and re-layouts: 1.14 us -> none
    pallas_call x1, Pallas kernels: 71.9 us -> 71 us  [shards(): pl.pallas_call(functools.partial(kernel, n_tile, n_spec, 3, GROUPS), out_...]
where the time goes in v6:
time: 73.9 us; the launch traced here: 73.7 us
  Pallas kernels  72.5 us (98%)
  between operations  1.18 us (2%)
    pallas_call x1, Pallas kernels, shards(): pl.pallas_call(functools.partial(kernel, n_tile, n_spec, 3, GROUPS), out_...  71 us
    pallas_call x1, Pallas kernels, shards(): pl.pallas_call(finish, out_shape=jax.ShapeDtypeStruct((total, cells), BF1...  1.54 us

profile of v6, /device:TPU:1, one launch (start us, length us, event | category | flops | bytes accessed | tf_op | source)
XLA Modules:
  0.0 73.7 jit_solution(14989803392689749941)
XLA Ops:
  0.6 71.0 %sweep_exchange_chemistry.1 = (bf16[192,4096]{1,0:T(8,128)(2,1)S(1)}, f32[1,1]{1,0:T(1,128)S(1)}, bf16[512,192]{1,0:T(8,128)(2,1)S(1)}, bf16[512,512]{1,0:T(8,12...) custom-call(f32[8,384,256]{2,1,0:T(8,128)} %conc.1, f32[384,256]{1,0:T(8,128)} %courant.1, ...), custom_call_target="tpu_custom_call" | custom-call | tf_op jit(solution)/shard_map/sweep_exchange_chemistry/pallas_call | solution.py:356
  72.2 1.5 %last_group.1 = bf16[192,4096]{1,0:T(8,128)(2,1)} custom-call(bf16[192,4096]{1,0:T(8,128)(2,1)S(1)} %get-tuple-element.8.part, bf16[512,192]{1,0:T(8,128)(2,1)S(1)} %get-tuple-element.9.w1_t, bf16[512,512]{1,0:T(8,128)(2,1)S(1)} %get-tuple-element.10.w2_t, bf16[192,512]{1,0:T(8,128)(2,1)S(1)} %get-tuple-element.11.w3_t, s32[4,8,128]{2,1,0:T(8,128)S(1)} %get-tuple-element.12.flags), custom_call_target="tpu_custom_call" | custom-call | tf_op jit(solution)/shard_map/last_group/pallas_call | solution.py:399

commit v7 on v6

--- a/solution.py
+++ b/solution.py
@@ -265,7 +265,9 @@
     lax.fori_loop(0, 2, edge, 0)
 
     def later(i, carry):
-        g, k = i // (n_spec - 1), i % (n_spec - 1) + 1
+        g, at_step = i // (n_spec - 1), i % (n_spec - 1)
+        crossing = n_spec - n_y
+        k = jnp.where(at_step < crossing, at_step + at_step // (n_z - 1) + 1, n_z * (at_step - crossing + 1))
         d = partner(k)
 
         @pl.when((k % n_y != 0) | (d == 0) | (d == n_spec - 1))

time: 73.9 us -> 73.9 us (level)
  no operation moved by 1% of the time
where the time goes in v7:
time: 73.9 us; the launch traced here: 73.7 us
  Pallas kernels  72.5 us (98%)
  between operations  1.18 us (2%)
    pallas_call x1, Pallas kernels, shards(): pl.pallas_call(functools.partial(kernel, n_tile, n_spec, 3, GROUPS), out_...  71 us
    pallas_call x1, Pallas kernels, shards(): pl.pallas_call(finish, out_shape=jax.ShapeDtypeStruct((total, cells), BF1...  1.54 us

profile of v7, /device:TPU:1, one launch (start us, length us, event | category | flops | bytes accessed | tf_op | source)
XLA Modules:
  0.0 73.7 jit_solution(7217473730642954793)
XLA Ops:
  0.6 71.0 %sweep_exchange_chemistry.1 = (bf16[192,4096]{1,0:T(8,128)(2,1)S(1)}, f32[1,1]{1,0:T(1,128)S(1)}, bf16[512,192]{1,0:T(8,128)(2,1)S(1)}, bf16[512,512]{1,0:T(8,12...) custom-call(f32[8,384,256]{2,1,0:T(8,128)} %conc.1, f32[384,256]{1,0:T(8,128)} %courant.1, ...), custom_call_target="tpu_custom_call" | custom-call | tf_op jit(solution)/shard_map/sweep_exchange_chemistry/pallas_call | solution.py:358
  72.2 1.5 %last_group.1 = bf16[192,4096]{1,0:T(8,128)(2,1)} custom-call(bf16[192,4096]{1,0:T(8,128)(2,1)S(1)} %get-tuple-element.8.part, bf16[512,192]{1,0:T(8,128)(2,1)S(1)} %get-tuple-element.9.w1_t, bf16[512,512]{1,0:T(8,128)(2,1)S(1)} %get-tuple-element.10.w2_t, bf16[192,512]{1,0:T(8,128)(2,1)S(1)} %get-tuple-element.11.w3_t, s32[4,8,128]{2,1,0:T(8,128)S(1)} %get-tuple-element.12.flags), custom_call_target="tpu_custom_call" | custom-call | tf_op jit(solution)/shard_map/last_group/pallas_call | solution.py:401
